TPU v7x, 512 devices: a whole 4x4x16 slice. The times are simulated.
512 devices in a mesh: dp: 2 (over x_lo), seq: 32 (over z, core), tensor: 8 (over y, x_hi).
Axes of the slice: x: 4 (x_hi: 2, x_lo: 2; x = x_hi * 2 + x_lo), y: 4, z: 16, core: 2. Of those that a mesh axis runs over, the one named last changes fastest.
Arguments:
- queries: bfloat16 [2, 4096, 3072], P('dp', 'seq', 'tensor'), may hold values from -24 to 24
- keys: bfloat16 [2, 8192, 3072], P('dp', 'seq', 'tensor'), may hold values from -8 to 8
- values: bfloat16 [2, 8192, 3072], P('dp', 'seq', 'tensor'), may hold values from -160 to 160
- grad_out: bfloat16 [2, 4096, 3072], P('dp', 'seq', 'tensor'), may hold values from -60 to 60
- gain: float32 [3072], P('tensor'), may hold values from 0.1 to 1.9
- band_start: int32 [2, 32], P('dp', 'seq'), may hold values from 0 to 62, as said below
- band_end: int32 [2, 32], P('dp', 'seq'), may hold values from 6 to 64
Outputs:
- attended: bfloat16 [2, 4096, 3072], P('dp', 'seq', 'tensor')
- grad_queries: bfloat16 [2, 4096, 3072], P('dp', 'seq', 'tensor')
- grad_keys: bfloat16 [2, 8192, 3072], P('dp', 'seq', 'tensor')
- grad_values: bfloat16 [2, 8192, 3072], P('dp', 'seq', 'tensor')
- grad_gain: float32 [3072], P('tensor')
Inputs may be any that keep to these rules, and one draw needn't show every extreme that they name: Along the token blocks of a recording band_start and band_end never fall and band_start < band_end; the band of a token block held by seq index j lies within encoder blocks (j - 2) * (2) to (j + 3) * 2 - 1, and in every draw some bands reach both of these limits.
All inputs are finite; a program needn't handle non-finite values.
Results may differ from a plain program's by a relative error of at most 0.008.
Values may be sent and summed in bfloat16 or wider, within the bound.
No kernel may reach another device: no remote copies, remote signals or barrier semaphores. Data moves between devices by JAX's collectives and lax.ppermute only.
A program may use at most 64 MiB of HBM per device.

v0:
```python
import jax
import jax.numpy as jnp
from jax import lax
from jax.experimental import pallas as pl
from jax.experimental.pallas import tpu as pltpu
from jax.sharding import PartitionSpec as P


D = 3072
HD = 96
TB = 128
EB = 128
FR = 256
W = 384
TENSOR = 8
SEQ = 32
SCALE = HD ** (-0.5)
epsilon = 1e-06

PIECES = 5
NT = (((1,), (1,)), ((), ()))
PAIRS = ((0, (0, 96)), (128, (64, 160)))


def permute(array, axis, target):
    size = lax.axis_size(axis)
    pairs = [(i, target(i)) for i in range(size) if 0 <= target(i) < size]
    return lax.ppermute(array, axis, pairs)


def offsets(here):
    core = lax.rem(here, 2)
    toward = 1 - 2 * core
    return (0, toward, -2, 2, -toward)


def blocked(rows, pair):
    first, starts = PAIRS[pair]
    part = rows[:, first : first + 256]
    lane = lax.broadcasted_iota(jnp.int32, part.shape, 1)
    zero = jnp.zeros_like(part)
    return jnp.concatenate(
        [jnp.where((lane >= at) & (lane < at + HD), part, zero) for at in starts], axis=0
    )


def side_by_side(pairs):
    lane = lax.broadcasted_iota(jnp.int32, (TB, 256), 1)
    low = jnp.where(lane < HD, pairs[0][:TB], pairs[0][TB:])
    high = jnp.where(lane < 160, pairs[1][:TB], pairs[1][TB:])
    middle = jnp.where(lane[:, :128] < 64, low[:, 128:], high[:, :128])
    return jnp.concatenate([low[:, :128], middle, high[:, 128:]], axis=1)


def to_rows(columns):
    lane = lax.broadcasted_iota(jnp.int32, (TB, TB), 1)
    tile = jnp.zeros((TB, TB), jnp.float32)
    for index, column in enumerate(columns):
        tile = jnp.where(lane == index, column, tile)
    return tile.T


def split(rows):
    terms = []
    for _ in range(3):
        term = rows.astype(jnp.bfloat16)
        rows = rows - term.astype(jnp.float32)
        terms.append(term)
    return jnp.concatenate(terms, axis=1)


def merge(terms):
    terms = terms.astype(jnp.float32)
    return (terms[:, 0:TB] + terms[:, TB : 2 * TB]) + terms[:, 2 * TB : W]


def pack_kernel(
    k_ref, v_ref, q_ref, go_ref, gain_ref, own_ref, query_ref, grad_ref, row_ref, line, sems
):
    moves = (
        (k_ref, own_ref.at[0:FR]),
        (v_ref, own_ref.at[FR : 2 * FR]),
        (q_ref, query_ref),
        (go_ref, grad_ref),
        (gain_ref, line),
    )
    copies = [
        pltpu.make_async_copy(source, target, sems.at[index])
        for index, (source, target) in enumerate(moves)
    ]
    for copy in copies:
        copy.start()
    for copy in copies:
        copy.wait()
    row_ref[...] = line[...].reshape(1, W)


def masked_scores(block, keys, frames, first, last):
    product = lax.dot_general(block, keys, NT, preferred_element_type=jnp.float32) * SCALE
    parts = []
    for half in range(2):
        allowed = (frames + half >= first) & (frames + half < last)
        parts.append(
            product[:, half * EB : (half + 1) * EB] + jnp.where(allowed, 0.0, -jnp.inf)
        )
    return parts


def score_kernel(start_ref, end_ref, q_ref, *rest):
    pieces = rest[: PIECES - 1]
    scores, tops_ref = rest[PIECES - 1 :]
    here = lax.axis_index("seq")
    rows = q_ref[...]
    for pair in range(2):
        at = PAIRS[pair][0]
        block = blocked(rows, pair)
        top = None
        for index, offset in enumerate(offsets(here)[: PIECES - 1]):
            parts = masked_scores(
                block,
                pieces[index][0:FR, at : at + 256],
                2 * (here + offset),
                start_ref[0, 0],
                end_ref[0, 0],
            )
            for half, part in enumerate(parts):
                scores[pair, :, index * FR + half * EB : index * FR + (half + 1) * EB] = part
                top = part if top is None else jnp.maximum(top, part)
        tops_ref[pair] = top


def forward_kernel(
    start_ref, end_ref, q_ref, go_ref, gain_ref, scores_ref, tops_ref, *rest
):
    pieces = rest[:PIECES]
    attn_ref, probs_ref, stats_ref, norms_ref = rest[PIECES:]
    here = lax.axis_index("seq")
    rows = q_ref[...]
    results = []
    tops = []
    scales = []
    for pair in range(2):
        at = PAIRS[pair][0]
        parts = masked_scores(
            blocked(rows, pair),
            pieces[-1][0:FR, at : at + 256],
            2 * (here + offsets(here)[-1]),
            start_ref[0, 0],
            end_ref[0, 0],
        )
        top = jnp.maximum(tops_ref[pair], jnp.maximum(parts[0], parts[1]))
        top = jnp.max(top, axis=1, keepdims=True)
        weights = jnp.concatenate(
            [jnp.exp(scores_ref[pair] - top), *[jnp.exp(part - top) for part in parts]], axis=1
        )
        total = jnp.sum(weights, axis=1, keepdims=True)
        inverse = 1.0 / total
        tops += [top[:TB], top[TB:]]
        scales += [inverse[:TB], inverse[TB:]]
        probs = weights * inverse
        probs_ref[pair] = probs
        probs = probs.astype(jnp.bfloat16)
        acc = None
        for index in range(PIECES):
            part = jnp.dot(
                probs[:, index * FR : (index + 1) * FR],
                pieces[index][FR : 2 * FR, at : at + 256],
                preferred_element_type=jnp.float32,
            )
            acc = part if acc is None else acc + part
        results.append(acc)
    attn = side_by_side(results)
    attn_ref[...] = attn
    scaled = go_ref[...].astype(jnp.float32) * gain_ref[...]
    square = jnp.sum(attn * attn, axis=1, keepdims=True)
    cross = jnp.sum(scaled * attn, axis=1, keepdims=True)
    stats = to_rows([*tops, *scales, square, cross])
    norms_ref[...] = stats[0:8]
    for index in range(TENSOR):
        stats_ref[index] = stats[8:10]


def token_kernel(
    start_ref, end_ref, q_ref, go_ref, gain_ref, attn_ref, probs_ref, norms_ref, stats_ref, *rest
):
    pieces = rest[:PIECES]
    attended_ref, gain_part_ref, gq_ref, sent_ref, grads = rest[PIECES:]
    stats = stats_ref[0]
    for index in range(1, TENSOR):
        stats = stats + stats_ref[index]
    row = lax.broadcasted_iota(jnp.int32, (TB, TB), 0)
    tile = jnp.where(row == 0, stats[0:1], jnp.where(row == 1, stats[1:2], 0.0)).T
    inv = lax.rsqrt(tile[:, 0:1] / D + epsilon)
    mean_cross = inv * tile[:, 1:2] / D
    grad = go_ref[...].astype(jnp.float32)
    gain = gain_ref[...]
    normed = attn_ref[...] * inv
    attended_ref[...] = (normed * gain).astype(jnp.bfloat16)
    gain_part_ref[...] = jnp.broadcast_to(
        jnp.sum(grad * normed, axis=0, keepdims=True)[None], (SEQ, 1, W)
    )
    grad_attn = (inv * (grad * gain - normed * mean_cross)).astype(jnp.bfloat16)
    sent_ref[0:TB] = grad_attn
    grad_q = []
    inners = []
    for pair in range(2):
        at = PAIRS[pair][0]
        cot = blocked(grad_attn, pair)
        inner = None
        for index in range(PIECES):
            span = slice(index * FR, (index + 1) * FR)
            part = lax.dot_general(
                cot,
                pieces[index][FR : 2 * FR, at : at + 256],
                NT,
                preferred_element_type=jnp.float32,
            )
            grads[:, span] = part
            part = probs_ref[pair, :, span] * part
            inner = part if inner is None else inner + part
        inner = jnp.sum(inner, axis=1, keepdims=True)
        inners += [inner[:TB], inner[TB:]]
        acc = None
        for index in range(PIECES):
            span = slice(index * FR, (index + 1) * FR)
            ds = (probs_ref[pair, :, span] * (grads[:, span] - inner)).astype(jnp.bfloat16)
            part = jnp.dot(
                ds, pieces[index][0:FR, at : at + 256], preferred_element_type=jnp.float32
            )
            acc = part if acc is None else acc + part
        grad_q.append(acc)
    gq_ref[...] = (side_by_side(grad_q) * SCALE).astype(jnp.bfloat16)
    band = lax.broadcasted_iota(jnp.int32, (4, TB), 0)
    band = jnp.where(band == 0, start_ref[0, 0], end_ref[0, 0]).astype(jnp.float32)
    sent_ref[TB : TB + 16] = split(
        jnp.concatenate([norms_ref[...], to_rows(inners)[0:4], band], axis=0)
    )


def frame_sums(kv_ref, here, tokens, queries):
    totals = []
    extras = [merge(token[TB : TB + 16]) for token in tokens]
    for pair in range(2):
        at = PAIRS[pair][0]
        keys = kv_ref[0:FR, at : at + 256]
        values = kv_ref[FR : 2 * FR, at : at + 256]
        grad_k = grad_v = None
        for index, extra in enumerate(extras):

            def both(base):
                low = base + 2 * pair
                return jnp.concatenate([extra[low : low + 1], extra[low + 1 : low + 2]], axis=1)

            top, inverse, inner = both(0), both(4), both(8)
            first = jnp.concatenate([extra[12:13]] * 2, axis=1)
            last = jnp.concatenate([extra[13:14]] * 2, axis=1)
            block = blocked(queries[index], pair)
            cot = blocked(tokens[index][0:TB], pair)
            scores = (
                lax.dot_general(keys, block, NT, preferred_element_type=jnp.float32) * SCALE
            )
            weights = []
            for half in range(2):
                frame = (2 * here + half).astype(jnp.float32)
                allowed = (frame >= first) & (frame < last)
                weights.append(
                    jnp.exp(scores[half * EB : (half + 1) * EB] - jnp.where(allowed, top, jnp.inf))
                )
            probs = jnp.concatenate(weights, axis=0) * inverse
            grads = lax.dot_general(values, cot, NT, preferred_element_type=jnp.float32)
            ds = (probs * (grads - inner)).astype(jnp.bfloat16)
            part_v = jnp.dot(
                probs.astype(jnp.bfloat16), cot, preferred_element_type=jnp.float32
            )
            part_k = jnp.dot(ds, block, preferred_element_type=jnp.float32)
            if grad_k is None:
                grad_k, grad_v = part_k, part_v
            else:
                grad_k, grad_v = grad_k + part_k, grad_v + part_v
        totals.append((grad_k, grad_v))
    return totals


def columns(totals, which):
    low, high = totals[0][which], totals[1][which]
    return ((0, low[:, :128]), (128, low[:, 128:] + high[:, :128]), (256, high[:, 128:]))


def partner_frame_kernel(
    kv_ref, sent_ref, below_ref, above_ref, q_ref, q_below_ref, q_above_ref, out_ref
):
    here = lax.axis_index("seq")
    core = lax.rem(here, 2)
    far = jnp.where(core == 0, above_ref[...], below_ref[...])
    q_far = jnp.where(core == 0, q_above_ref[...], q_below_ref[...])
    totals = frame_sums(
        kv_ref, here + 1 - 2 * core, (sent_ref[...], far), (q_ref[...], q_far)
    )
    for which in range(2):
        for at, part in columns(totals, which):
            out_ref[which * FR : (which + 1) * FR, at : at + 128] = part.astype(out_ref.dtype)


def own_frame_kernel(
    kv_ref,
    sent_ref,
    below_ref,
    above_ref,
    q_ref,
    q_below_ref,
    q_above_ref,
    more_ref,
    gk_ref,
    gv_ref,
):
    tokens = (sent_ref[...], below_ref[...], above_ref[...])
    queries = (q_ref[...], q_below_ref[...], q_above_ref[...])
    totals = frame_sums(kv_ref, lax.axis_index("seq"), tokens, queries)
    for which, (out, scale) in enumerate(((gk_ref, SCALE), (gv_ref, 1.0))):
        for at, part in columns(totals, which):
            more = more_ref[which * FR : (which + 1) * FR, at : at + 128].astype(jnp.float32)
            out[:, at : at + 128] = ((part + more) * scale).astype(out.dtype)


VMEM = pl.BlockSpec(memory_space=pltpu.VMEM)
SMEM = pl.BlockSpec(memory_space=pltpu.SMEM)


def call(kernel, outputs, products, scratch=(), scalars=0, vectors=0):
    return pl.pallas_call(
        kernel,
        out_shape=tuple(jax.ShapeDtypeStruct(shape, dtype) for shape, dtype in outputs),
        in_specs=[SMEM] * scalars + [VMEM] * vectors,
        out_specs=(VMEM,) * len(outputs),
        scratch_shapes=[pltpu.VMEM(shape, jnp.float32) for shape in scratch],
        compiler_params=pltpu.CompilerParams(vmem_limit_bytes=24 << 20),
        cost_estimate=pl.CostEstimate(
            flops=products * 2 * 512 * 1280 * 256,
            bytes_accessed=4 << 20,
            transcendentals=512 * 1280,
        ),
    )


def per_device(queries, keys, values, grad_out, gain, band_start, band_end):
    f32, bf16 = jnp.float32, jnp.bfloat16
    here = lax.axis_index("seq")
    core = lax.rem(here, 2)
    own, query, grad, gain_row = pl.pallas_call(
        pack_kernel,
        out_shape=(
            jax.ShapeDtypeStruct((2 * FR, W), bf16),
            jax.ShapeDtypeStruct((TB, W), bf16),
            jax.ShapeDtypeStruct((TB, W), bf16),
            jax.ShapeDtypeStruct((1, W), f32),
        ),
        in_specs=[pl.BlockSpec(memory_space=pltpu.HBM)] * 5,
        out_specs=(VMEM,) * 4,
        scratch_shapes=[pltpu.VMEM((W,), f32), pltpu.SemaphoreType.DMA((5,))],
        compiler_params=pltpu.CompilerParams(vmem_limit_bytes=24 << 20),
        name="pack",
    )(*[
        pltpu.with_memory_space_constraint(array, pltpu.HBM)
        for array in (keys[0], values[0], queries[0], grad_out[0], gain)
    ])
    below = permute(own, "seq", lambda i: i + 2)
    above = permute(own, "seq", lambda i: i - 2)
    partner = permute(own, "seq", lambda i: i ^ 1)
    asked = (query, permute(query, "seq", lambda i: i + 2), permute(query, "seq", lambda i: i - 2))
    whole = (2 * TB, PIECES * FR)
    beyond = permute(jnp.where(core == 0, above, below), "seq", lambda i: i ^ 1)
    pieces = (own, partner, below, above, beyond)
    scores, tops = call(
        score_kernel,
        (((2, 2 * TB, (PIECES - 1) * FR), f32), ((2, 2 * TB, EB), f32)),
        1,
        scalars=2,
        vectors=PIECES,
    )(band_start, band_end, query, *pieces[:-1])
    attn, probs, stats, norms = call(
        forward_kernel,
        (((TB, W), f32), ((2, *whole), f32), ((TENSOR, 2, TB), f32), ((8, TB), f32)),
        1,
        scalars=2,
        vectors=5 + PIECES,
    )(band_start, band_end, query, grad, gain_row, scores, tops, *pieces)
    stats = lax.all_to_all(stats, "tensor", 0, 0, tiled=False)
    attended, gain_part, grad_queries, sent = call(
        token_kernel,
        (((TB, W), bf16), ((SEQ, 1, W), f32), ((TB, W), bf16), ((TB + 16, W), bf16)),
        2,
        scratch=(whole,),
        scalars=2,
        vectors=7 + PIECES,
    )(band_start, band_end, query, grad, gain_row, attn, probs, norms, stats, *pieces)
    spread = lax.all_to_all(gain_part, "seq", 0, 0, tiled=False)
    gain_sum = jnp.sum(spread, axis=(0, 1))
    tokens = (sent, permute(sent, "seq", lambda i: i + 2), permute(sent, "seq", lambda i: i - 2))
    (to_partner,) = call(
        partner_frame_kernel, (((2 * FR, W), bf16),), 2, vectors=7
    )(partner, *tokens, *asked)
    from_partner = permute(to_partner, "seq", lambda i: i ^ 1)
    gain_other = lax.ppermute(gain_sum, "dp", [(0, 1), (1, 0)])
    grad_keys, grad_values = call(
        own_frame_kernel, (((FR, W), bf16), ((FR, W), bf16)), 2, vectors=8
    )(own, *tokens, *asked, from_partner)
    grad_gain = gain_sum + gain_other
    return (
        attended[None],
        grad_queries[None],
        grad_keys[None],
        grad_values[None],
        grad_gain,
    )


def solution(mesh):
    return jax.shard_map(
        per_device,
        mesh=mesh,
        in_specs=(
            P("dp", "seq", "tensor"),
            P("dp", "seq", "tensor"),
            P("dp", "seq", "tensor"),
            P("dp", "seq", "tensor"),
            P("tensor"),
            P("dp", "seq"),
            P("dp", "seq"),
        ),
        out_specs=(
            P("dp", "seq", "tensor"),
            P("dp", "seq", "tensor"),
            P("dp", "seq", "tensor"),
            P("dp", "seq", "tensor"),
            P("tensor"),
        ),
        check_vma=False,
    )
```

profile of v0, /device:TPU:2, one launch (start us, length us, event | category | flops | bytes accessed | tf_op | source)
XLA Modules:
  0.0 95.9 jit_solution(15794282467774824112)
XLA Ops:
  0.6 1.2 %pack.1 = (bf16[512,384]{1,0:T(8,128)(2,1)S(1)}, bf16[128,384]{1,0:T(8,128)(2,1)S(1)}, bf16[128,384]{1,0:T(8,128)(2,1)S(1)}, f32[1,384]{1,0:T(1,128)S(1)}) custom-call(bf16[256,384]{1,0:T(8,128)(2,1)} %bitcast.8, bf16[256,384]{1,0:T(8,128)(2,1)} %bitcast.9, bf16[128,384]{1,0:T(8,128)(2,1)} %bitcast.10, bf16[128,384]{1,0:T(8,128)(2,1)} %bitcast.11, f32[384]{0:T(512)} %gain_ref.1), custom_call_target="tpu_custom_call" | custom-call | tf_op jit(solution)/shard_map/pack/pallas_call | solution.py:349
  1.8 3.8 %collective-permute-start.1 = (bf16[512,384]{1,0:T(8,128)(2,1)S(1)}, bf16[512,384]{1,0:T(8,128)(2,1)S(1)}, u32[]{:S(2)}, u32[]{:S(2)}) collective-permute-start(bf16[512,384]{1,0:T(8,128)(2,1)S(1)} %get-tuple-element.24.rest_0_.kv_ref), channel_id=1, source_target_pairs={{0,16},{8,24},{16,32},{24,40},{32,48},{40,56},{48,64},{56,72},{64,... | collective-permute-start | bytes 1179656 | tf_op jit(solution)/shard_map/ppermute | solution.py:28
  5.7 1.3 %collective-permute-start.2 = (bf16[512,384]{1,0:T(8,128)(2,1)S(1)}, bf16[512,384]{1,0:T(8,128)(2,1)S(1)}, u32[]{:S(2)}, u32[]{:S(2)}) collective-permute-start(bf16[512,384]{1,0:T(8,128)(2,1)S(1)} %get-tuple-element.24.rest_0_.kv_ref), channel_id=1, source_target_pairs={{16,0},{24,8},{32,16},{40,24},{48,32},{56,40},{64,48},{72,56},{80,... | collective-permute-start | bytes 1179656 | tf_op jit(solution)/shard_map/ppermute | solution.py:28
  7.0 1.9 %collective-permute-start = (bf16[512,384]{1,0:T(8,128)(2,1)S(1)}, bf16[512,384]{1,0:T(8,128)(2,1)S(1)}, u32[]{:S(2)}, u32[]{:S(2)}) collective-permute-start(bf16[512,384]{1,0:T(8,128)(2,1)S(1)} %get-tuple-element.24.rest_0_.kv_ref), channel_id=1, source_target_pairs={{0,8},{8,0},{16,24},{24,16},{32,40},{40,32},{48,56},{56,48},{64,72... | collective-permute-start | bytes 1179656 | tf_op jit(solution)/shard_map/ppermute | solution.py:28
  8.9 5.1 %collective-permute-done.1.rest_2_ = bf16[512,384]{1,0:T(8,128)(2,1)S(1)} collective-permute-done((bf16[512,384]{1,0:T(8,128)(2,1)S(1)}, bf16[512,384]{1,0:T(8,128)(2,1)S(1)}, u32[]{:S(2)}, u32[]{:S(2)}) %collective-permute-start.1) | collective-permute-done | bytes 393248 | tf_op jit(solution)/shard_map/ppermute | solution.py:28
  14.0 4.3 %collective-permute-done.2.rest_3_ = bf16[512,384]{1,0:T(8,128)(2,1)S(1)} collective-permute-done((bf16[512,384]{1,0:T(8,128)(2,1)S(1)}, bf16[512,384]{1,0:T(8,128)(2,1)S(1)}, u32[]{:S(2)}, u32[]{:S(2)}) %collective-permute-start.2) | collective-permute-done | bytes 393248 | tf_op jit(solution)/shard_map/ppermute | solution.py:28
  18.4 1.9 %collective-permute-start.3 = (bf16[512,384]{1,0:T(8,128)(2,1)S(1)}, bf16[512,384]{1,0:T(8,128)(2,1)S(1)}, u32[]{:S(2)}, u32[]{:S(2)}) collective-permute-start(bf16[512,384]{1,0:T(8,128)(2,1)S(1)} %broadcast_select_fusion), channel_id=1, source_target_pairs={{0,8},{8,0},{16,24},{24,16},{32,40},{40,32},{48,56},{56,48},{64,72... | collective-permute-start | bytes 1179656 | tf_op jit(solution)/shard_map/ppermute | solution.py:28
  21.6 0.0 collective-permute-done.rest_1_.kv_ref
  21.6 0.5 shard_map.110
  22.1 0.0 collective-permute-done.3.rest_4_
  22.1 1.4 %shard_map.111 = (f32[128,384]{1,0:T(8,128)S(1)}, f32[2,256,1280]{2,1,0:T(8,128)S(1)}, f32[8,2,128]{2,1,0:T(2,128)S(1)}, f32[8,128]{1,0:T(8,128)S(1)}) custom-call(s32[1,1]{1,0:T(1,128)S(6)} %copy.12.start_ref, s32[1,1]{1,0:T(1,128)S(6)} %copy.13.end_ref, bf16[128,384]{1,0:T(8,128)(2,1)S(1)} %get-tuple-element.21.q_ref, ...), custom_call_target="tpu_custom_call" | custom-call | flops 335544320 | bytes 4194304 | tf_op jit(solution)/shard_map/pallas_call | solution.py:380
  23.5 13.5 %all_to_all.10.stats_ref = f32[8,2,128]{2,1,0:T(2,128)S(1)} all-to-all(f32[8,2,128]{2,1,0:T(2,128)S(1)} %get-tuple-element.30), channel_id=1, replica_groups=mesh['dp'=2,'seq'=32,'tensor'=8] {'tensor'}, dimensions={0} | all-to-all | bytes 16384 | tf_op jit(solution)/shard_map/all_to_all | solution.py:387
  37.0 2.3 %shard_map.112 = (bf16[128,384]{1,0:T(8,128)(2,1)}, f32[32,1,384]{2,1,0:T(1,128)S(1)}, bf16[128,384]{1,0:T(8,128)(2,1)}, bf16[144,384]{1,0:T(8,128)(2,1)S(1)}) custom-call(s32[1,1]{1,0:T(1,128)S(6)} %copy.12.start_ref, s32[1,1]{1,0:T(1,128)S(6)} %copy.13.end_ref, bf16[128,384]{1,0:T(8,128)(2,1)S(1)} %get-tuple-element.21.q_ref, ...), custom_call_target="tpu_custom_call" | custom-call | flops 671088640 | bytes 4194304 | tf_op jit(solution)/shard_map/pallas_call | solution.py:388
  39.3 3.8 %collective-permute-start.4 = (bf16[144,384]{1,0:T(8,128)(2,1)S(1)}, bf16[144,384]{1,0:T(8,128)(2,1)S(1)}, u32[]{:S(2)}, u32[]{:S(2)}) collective-permute-start(bf16[144,384]{1,0:T(8,128)(2,1)S(1)} %get-tuple-element.33.sent_ref), channel_id=1, source_target_pairs={{0,16},{8,24},{16,32},{24,40},{32,48},{40,56},{48,64},{56,72},{64,... | collective-permute-start | bytes 331784 | tf_op jit(solution)/shard_map/ppermute | solution.py:28
  43.1 1.3 %collective-permute-start.5 = (bf16[144,384]{1,0:T(8,128)(2,1)S(1)}, bf16[144,384]{1,0:T(8,128)(2,1)S(1)}, u32[]{:S(2)}, u32[]{:S(2)}) collective-permute-start(bf16[144,384]{1,0:T(8,128)(2,1)S(1)} %get-tuple-element.33.sent_ref), channel_id=1, source_target_pairs={{16,0},{24,8},{32,16},{40,24},{48,32},{56,40},{64,48},{72,56},{80,... | collective-permute-start | bytes 331784 | tf_op jit(solution)/shard_map/ppermute | solution.py:28
  44.4 5.7 %collective-permute-start.6 = (bf16[128,384]{1,0:T(8,128)(2,1)S(1)}, bf16[128,384]{1,0:T(8,128)(2,1)S(1)}, u32[]{:S(2)}, u32[]{:S(2)}) collective-permute-start(bf16[128,384]{1,0:T(8,128)(2,1)S(1)} %get-tuple-element.21.q_ref), channel_id=1, source_target_pairs={{0,16},{8,24},{16,32},{24,40},{32,48},{40,56},{48,64},{56,72},{64,... | collective-permute-start | bytes 294920 | tf_op jit(solution)/shard_map/ppermute | solution.py:28
  50.1 1.3 %collective-permute-start.7 = (bf16[128,384]{1,0:T(8,128)(2,1)S(1)}, bf16[128,384]{1,0:T(8,128)(2,1)S(1)}, u32[]{:S(2)}, u32[]{:S(2)}) collective-permute-start(bf16[128,384]{1,0:T(8,128)(2,1)S(1)} %get-tuple-element.21.q_ref), channel_id=1, source_target_pairs={{16,0},{24,8},{32,16},{40,24},{48,32},{56,40},{64,48},{72,56},{80,... | collective-permute-start | bytes 294920 | tf_op jit(solution)/shard_map/ppermute | solution.py:28
  51.4 0.9 collective-permute-done.6.q_below_ref
  52.3 5.3 %collective-permute-done.7.q_above_ref = bf16[128,384]{1,0:T(8,128)(2,1)S(1)} collective-permute-done((bf16[128,384]{1,0:T(8,128)(2,1)S(1)}, bf16[128,384]{1,0:T(8,128)(2,1)S(1)}, u32[]{:S(2)}, u32[]{:S(2)}) %collective-permute-start.7) | collective-permute-done | bytes 98336 | tf_op jit(solution)/shard_map/ppermute | solution.py:28
  57.5 0.0 collective-permute-done.4.below_ref
  57.5 0.0 collective-permute-done.5.above_ref
  57.5 1.0 shard_map.113
  58.5 1.9 %collective-permute-start.8 = (bf16[512,384]{1,0:T(8,128)(2,1)S(1)}, bf16[512,384]{1,0:T(8,128)(2,1)S(1)}, u32[]{:S(2)}, u32[]{:S(2)}) collective-permute-start(bf16[512,384]{1,0:T(8,128)(2,1)S(1)} %shard_map.113), channel_id=1, source_target_pairs={{0,8},{8,0},{16,24},{24,16},{32,40},{40,32},{48,56},{56,48},{64,72... | collective-permute-start | bytes 1179656 | tf_op jit(solution)/shard_map/ppermute | solution.py:28
  60.4 27.2 %all_to_all.11 = f32[32,1,384]{2,1,0:T(1,128)S(1)} all-to-all(f32[32,1,384]{2,1,0:T(1,128)S(1)} %get-tuple-element.36), channel_id=1, replica_groups=mesh['dp'=2,'seq'=32,'tensor'=8] {'seq'}, dimensions={0} | all-to-all | bytes 98304 | tf_op jit(solution)/shard_map/all_to_all | solution.py:396
  87.6 0.1 reduce_sum.9
  87.7 3.3 %collective-permute-start.9 = (f32[384]{0:T(512)S(1)}, f32[384]{0:T(512)S(1)}, u32[]{:S(2)}, u32[]{:S(2)}) collective-permute-start(f32[384]{0:T(512)S(1)} %reduce_sum.9), channel_id=1, source_target_pairs={{0,256},{256,0},{1,257},{257,1},{2,258},{258,2},{3,259},{259,3},{4... | collective-permute-start | bytes 4616 | tf_op jit(solution)/shard_map/ppermute | solution.py:403
  91.0 2.1 %collective-permute-done.9 = f32[384]{0:T(512)S(1)} collective-permute-done((f32[384]{0:T(512)S(1)}, f32[384]{0:T(512)S(1)}, u32[]{:S(2)}, u32[]{:S(2)}) %collective-permute-start.9) | collective-permute-done | bytes 1568 | tf_op jit(solution)/shard_map/ppermute | solution.py:403
  93.2 0.6 add.3
  93.7 0.0 collective-permute-done.8.more_ref
  93.7 2.1 %shard_map.114 = (bf16[256,384]{1,0:T(8,128)(2,1)}, bf16[256,384]{1,0:T(8,128)(2,1)}) custom-call(bf16[512,384]{1,0:T(8,128)(2,1)S(1)} %get-tuple-element.24.rest_0_.kv_ref, bf16[144,384]{1,0:T(8,128)(2,1)S(1)} %get-tuple-element.33.sent_ref, bf16[144,384]{1,0:T(8,128)(2,1)S(1)} %collective-permute-done.4.below_ref, ...), custom_call_target="tpu_custom_call" | custom-call | flops 671088640 | bytes 4194304 | tf_op jit(solution)/shard_map/pallas_call | solution.py:404
  (1 shorter events, 0.0 us)
Async XLA Ops:
  1.8 12.2 %collective-permute-start.1 = (bf16[512,384]{1,0:T(8,128)(2,1)S(1)}, bf16[512,384]{1,0:T(8,128)(2,1)S(1)}, u32[]{:S(2)}, u32[]{:S(2)}) collective-permute-start(bf16[512,384]{1,0:T(8,128)(2,1)S(1)} %get-tuple-element.24.rest_0_.kv_ref), channel_id=1, source_target_pairs={{0,16},{8,24},{16,32},{24,40},{32,48},{40,56},{48,64},{56,72},{64,... | collective-permute-start | bytes 1179656 | tf_op jit(solution)/shard_map/ppermute | solution.py:28
  5.7 12.6 %collective-permute-start.2 = (bf16[512,384]{1,0:T(8,128)(2,1)S(1)}, bf16[512,384]{1,0:T(8,128)(2,1)S(1)}, u32[]{:S(2)}, u32[]{:S(2)}) collective-permute-start(bf16[512,384]{1,0:T(8,128)(2,1)S(1)} %get-tuple-element.24.rest_0_.kv_ref), channel_id=1, source_target_pairs={{16,0},{24,8},{32,16},{40,24},{48,32},{56,40},{64,48},{72,56},{80,... | collective-permute-start | bytes 1179656 | tf_op jit(solution)/shard_map/ppermute | solution.py:28
  7.0 14.6 %collective-permute-start = (bf16[512,384]{1,0:T(8,128)(2,1)S(1)}, bf16[512,384]{1,0:T(8,128)(2,1)S(1)}, u32[]{:S(2)}, u32[]{:S(2)}) collective-permute-start(bf16[512,384]{1,0:T(8,128)(2,1)S(1)} %get-tuple-element.24.rest_0_.kv_ref), channel_id=1, source_target_pairs={{0,8},{8,0},{16,24},{24,16},{32,40},{40,32},{48,56},{56,48},{64,72... | collective-permute-start | bytes 1179656 | tf_op jit(solution)/shard_map/ppermute | solution.py:28
  18.4 3.7 %collective-permute-start.3 = (bf16[512,384]{1,0:T(8,128)(2,1)S(1)}, bf16[512,384]{1,0:T(8,128)(2,1)S(1)}, u32[]{:S(2)}, u32[]{:S(2)}) collective-permute-start(bf16[512,384]{1,0:T(8,128)(2,1)S(1)} %broadcast_select_fusion), channel_id=1, source_target_pairs={{0,8},{8,0},{16,24},{24,16},{32,40},{40,32},{48,56},{56,48},{64,72... | collective-permute-start | bytes 1179656 | tf_op jit(solution)/shard_map/ppermute | solution.py:28
  39.3 18.2 %collective-permute-start.4 = (bf16[144,384]{1,0:T(8,128)(2,1)S(1)}, bf16[144,384]{1,0:T(8,128)(2,1)S(1)}, u32[]{:S(2)}, u32[]{:S(2)}) collective-permute-start(bf16[144,384]{1,0:T(8,128)(2,1)S(1)} %get-tuple-element.33.sent_ref), channel_id=1, source_target_pairs={{0,16},{8,24},{16,32},{24,40},{32,48},{40,56},{48,64},{56,72},{64,... | collective-permute-start | bytes 331784 | tf_op jit(solution)/shard_map/ppermute | solution.py:28
  43.1 14.4 %collective-permute-start.5 = (bf16[144,384]{1,0:T(8,128)(2,1)S(1)}, bf16[144,384]{1,0:T(8,128)(2,1)S(1)}, u32[]{:S(2)}, u32[]{:S(2)}) collective-permute-start(bf16[144,384]{1,0:T(8,128)(2,1)S(1)} %get-tuple-element.33.sent_ref), channel_id=1, source_target_pairs={{16,0},{24,8},{32,16},{40,24},{48,32},{56,40},{64,48},{72,56},{80,... | collective-permute-start | bytes 331784 | tf_op jit(solution)/shard_map/ppermute | solution.py:28
  44.4 7.9 %collective-permute-start.6 = (bf16[128,384]{1,0:T(8,128)(2,1)S(1)}, bf16[128,384]{1,0:T(8,128)(2,1)S(1)}, u32[]{:S(2)}, u32[]{:S(2)}) collective-permute-start(bf16[128,384]{1,0:T(8,128)(2,1)S(1)} %get-tuple-element.21.q_ref), channel_id=1, source_target_pairs={{0,16},{8,24},{16,32},{24,40},{32,48},{40,56},{48,64},{56,72},{64,... | collective-permute-start | bytes 294920 | tf_op jit(solution)/shard_map/ppermute | solution.py:28
  50.1 7.4 %collective-permute-start.7 = (bf16[128,384]{1,0:T(8,128)(2,1)S(1)}, bf16[128,384]{1,0:T(8,128)(2,1)S(1)}, u32[]{:S(2)}, u32[]{:S(2)}) collective-permute-start(bf16[128,384]{1,0:T(8,128)(2,1)S(1)} %get-tuple-element.21.q_ref), channel_id=1, source_target_pairs={{16,0},{24,8},{32,16},{40,24},{48,32},{56,40},{64,48},{72,56},{80,... | collective-permute-start | bytes 294920 | tf_op jit(solution)/shard_map/ppermute | solution.py:28
  58.5 35.2 %collective-permute-start.8 = (bf16[512,384]{1,0:T(8,128)(2,1)S(1)}, bf16[512,384]{1,0:T(8,128)(2,1)S(1)}, u32[]{:S(2)}, u32[]{:S(2)}) collective-permute-start(bf16[512,384]{1,0:T(8,128)(2,1)S(1)} %shard_map.113), channel_id=1, source_target_pairs={{0,8},{8,0},{16,24},{24,16},{32,40},{40,32},{48,56},{56,48},{64,72... | collective-permute-start | bytes 1179656 | tf_op jit(solution)/shard_map/ppermute | solution.py:28
  87.7 5.5 %collective-permute-start.9 = (f32[384]{0:T(512)S(1)}, f32[384]{0:T(512)S(1)}, u32[]{:S(2)}, u32[]{:S(2)}) collective-permute-start(f32[384]{0:T(512)S(1)} %reduce_sum.9), channel_id=1, source_target_pairs={{0,256},{256,0},{1,257},{257,1},{2,258},{258,2},{3,259},{259,3},{4... | collective-permute-start | bytes 4616 | tf_op jit(solution)/shard_map/ppermute | solution.py:403
where the time goes:
time: 96.3 us; the launch traced here: 95.9 us
  blocking collectives  40.7 us (42%)
  starting transfers between devices  26.3 us (27%)
  waiting for transfers between devices  17.7 us (18%)
  Pallas kernels  8.41 us (9%)
  between operations  2.06 us (2%)
    all_to_all x1, blocking collectives, per_device(): spread = lax.all_to_all(gain_part, 'seq', 0, 0, tiled=False)  27.2 us
    ppermute x9, starting transfers between devices, permute(): return lax.ppermute(array, axis, pairs)  23 us
    ppermute x9, waiting for transfers between devices, permute(): return lax.ppermute(array, axis, pairs)  15.6 us
    all_to_all x1, blocking collectives, per_device(): stats = lax.all_to_all(stats, 'tensor', 0, 0, tiled=False)  13.5 us
    ppermute x1, starting transfers between devices, per_device(): gain_other = lax.ppermute(gain_sum, 'dp', [(0, 1), (1, 0)])  3.35 us
    pallas_call x1, Pallas kernels, per_device(): call(token_kernel, (((TB, W), bf16), ((SEQ, 1, W), f32), ((TB, W), bf16),...  2.26 us
    pallas_call x1, Pallas kernels, per_device(): call(own_frame_kernel, (((FR, W), bf16), ((FR, W), bf16)), 2, vectors=8)  2.12 us
    ppermute x1, waiting for transfers between devices, per_device(): gain_other = lax.ppermute(gain_sum, 'dp', [(0, 1), (1, 0)])  2.12 us
  transfers between devices with their start and end apart: 10, of which 5 were waited for; matrix products, arithmetic and copies ran while one was open for 1% of the time, Pallas kernels for 0%

commit v1 on v0

--- a/solution.py
+++ b/solution.py
@@ -200,7 +200,9 @@
         jnp.sum(grad * normed, axis=0, keepdims=True)[None], (SEQ, 1, W)
     )
     grad_attn = (inv * (grad * gain - normed * mean_cross)).astype(jnp.bfloat16)
+    rows = q_ref[...]
     sent_ref[0:TB] = grad_attn
+    sent_ref[TB : 2 * TB] = rows
     grad_q = []
     inners = []
     for pair in range(2):
@@ -232,14 +234,14 @@
     gq_ref[...] = (side_by_side(grad_q) * SCALE).astype(jnp.bfloat16)
     band = lax.broadcasted_iota(jnp.int32, (4, TB), 0)
     band = jnp.where(band == 0, start_ref[0, 0], end_ref[0, 0]).astype(jnp.float32)
-    sent_ref[TB : TB + 16] = split(
+    sent_ref[2 * TB : 2 * TB + 16] = split(
         jnp.concatenate([norms_ref[...], to_rows(inners)[0:4], band], axis=0)
     )
 
 
-def frame_sums(kv_ref, here, tokens, queries):
+def frame_sums(kv_ref, here, tokens):
     totals = []
-    extras = [merge(token[TB : TB + 16]) for token in tokens]
+    extras = [merge(token[2 * TB : 2 * TB + 16]) for token in tokens]
     for pair in range(2):
         at = PAIRS[pair][0]
         keys = kv_ref[0:FR, at : at + 256]
@@ -254,7 +256,7 @@
             top, inverse, inner = both(0), both(4), both(8)
             first = jnp.concatenate([extra[12:13]] * 2, axis=1)
             last = jnp.concatenate([extra[13:14]] * 2, axis=1)
-            block = blocked(queries[index], pair)
+            block = blocked(tokens[index][TB : 2 * TB], pair)
             cot = blocked(tokens[index][0:TB], pair)
             scores = (
                 lax.dot_general(keys, block, NT, preferred_element_type=jnp.float32) * SCALE
@@ -286,36 +288,19 @@
     return ((0, low[:, :128]), (128, low[:, 128:] + high[:, :128]), (256, high[:, 128:]))
 
 
-def partner_frame_kernel(
-    kv_ref, sent_ref, below_ref, above_ref, q_ref, q_below_ref, q_above_ref, out_ref
-):
+def partner_frame_kernel(kv_ref, sent_ref, below_ref, above_ref, out_ref):
     here = lax.axis_index("seq")
     core = lax.rem(here, 2)
     far = jnp.where(core == 0, above_ref[...], below_ref[...])
-    q_far = jnp.where(core == 0, q_above_ref[...], q_below_ref[...])
-    totals = frame_sums(
-        kv_ref, here + 1 - 2 * core, (sent_ref[...], far), (q_ref[...], q_far)
-    )
+    totals = frame_sums(kv_ref, here + 1 - 2 * core, (sent_ref[...], far))
     for which in range(2):
         for at, part in columns(totals, which):
             out_ref[which * FR : (which + 1) * FR, at : at + 128] = part.astype(out_ref.dtype)
 
 
-def own_frame_kernel(
-    kv_ref,
-    sent_ref,
-    below_ref,
-    above_ref,
-    q_ref,
-    q_below_ref,
-    q_above_ref,
-    more_ref,
-    gk_ref,
-    gv_ref,
-):
+def own_frame_kernel(kv_ref, sent_ref, below_ref, above_ref, more_ref, gk_ref, gv_ref):
     tokens = (sent_ref[...], below_ref[...], above_ref[...])
-    queries = (q_ref[...], q_below_ref[...], q_above_ref[...])
-    totals = frame_sums(kv_ref, lax.axis_index("seq"), tokens, queries)
+    totals = frame_sums(kv_ref, lax.axis_index("seq"), tokens)
     for which, (out, scale) in enumerate(((gk_ref, SCALE), (gv_ref, 1.0))):
         for at, part in columns(totals, which):
             more = more_ref[which * FR : (which + 1) * FR, at : at + 128].astype(jnp.float32)
@@ -366,7 +351,6 @@
     below = permute(own, "seq", lambda i: i + 2)
     above = permute(own, "seq", lambda i: i - 2)
     partner = permute(own, "seq", lambda i: i ^ 1)
-    asked = (query, permute(query, "seq", lambda i: i + 2), permute(query, "seq", lambda i: i - 2))
     whole = (2 * TB, PIECES * FR)
     beyond = permute(jnp.where(core == 0, above, below), "seq", lambda i: i ^ 1)
     pieces = (own, partner, below, above, beyond)
@@ -387,7 +371,7 @@
     stats = lax.all_to_all(stats, "tensor", 0, 0, tiled=False)
     attended, gain_part, grad_queries, sent = call(
         token_kernel,
-        (((TB, W), bf16), ((SEQ, 1, W), f32), ((TB, W), bf16), ((TB + 16, W), bf16)),
+        (((TB, W), bf16), ((SEQ, 1, W), f32), ((TB, W), bf16), ((2 * TB + 16, W), bf16)),
         2,
         scratch=(whole,),
         scalars=2,
@@ -395,15 +379,17 @@
     )(band_start, band_end, query, grad, gain_row, attn, probs, norms, stats, *pieces)
     spread = lax.all_to_all(gain_part, "seq", 0, 0, tiled=False)
     gain_sum = jnp.sum(spread, axis=(0, 1))
-    tokens = (sent, permute(sent, "seq", lambda i: i + 2), permute(sent, "seq", lambda i: i - 2))
+    tokens_below = permute(sent, "seq", lambda i: i + 2)
+    tokens_above = permute(sent, "seq", lambda i: i - 2)
+    tokens = (sent, tokens_below, tokens_above)
     (to_partner,) = call(
-        partner_frame_kernel, (((2 * FR, W), bf16),), 2, vectors=7
-    )(partner, *tokens, *asked)
+        partner_frame_kernel, (((2 * FR, W), bf16),), 2, vectors=4
+    )(partner, *tokens)
     from_partner = permute(to_partner, "seq", lambda i: i ^ 1)
     gain_other = lax.ppermute(gain_sum, "dp", [(0, 1), (1, 0)])
     grad_keys, grad_values = call(
-        own_frame_kernel, (((FR, W), bf16), ((FR, W), bf16)), 2, vectors=8
-    )(own, *tokens, *asked, from_partner)
+        own_frame_kernel, (((FR, W), bf16), ((FR, W), bf16)), 2, vectors=5
+    )(own, *tokens, from_partner)
     grad_gain = gain_sum + gain_other
     return (
         attended[None],

time: 96.3 us -> 90.5 us (0.940)
  the two profiles are of different devices: /device:TPU:2 before, /device:TPU:6 now
where the time goes in v1:
time: 90.5 us; the launch traced here: 88.8 us
  blocking collectives  44 us (49%)
  starting transfers between devices  20.7 us (23%)
  waiting for transfers between devices  12.9 us (14%)
  Pallas kernels  8.41 us (9%)
  between operations  2.04 us (2%)
    all_to_all x1, blocking collectives, per_device(): spread = lax.all_to_all(gain_part, 'seq', 0, 0, tiled=False)  32 us
    ppermute x7, starting transfers between devices, permute(): return lax.ppermute(array, axis, pairs)  17.9 us
    all_to_all x1, blocking collectives, per_device(): stats = lax.all_to_all(stats, 'tensor', 0, 0, tiled=False)  12 us
    ppermute x7, waiting for transfers between devices, permute(): return lax.ppermute(array, axis, pairs)  10.2 us
    ppermute x1, starting transfers between devices, per_device(): gain_other = lax.ppermute(gain_sum, 'dp', [(0, 1), (1, 0)])  2.75 us
    ppermute x1, waiting for transfers between devices, per_device(): gain_other = lax.ppermute(gain_sum, 'dp', [(0, 1), (1, 0)])  2.72 us
    pallas_call x1, Pallas kernels, per_device(): call(token_kernel, (((TB, W), bf16), ((SEQ, 1, W), f32), ((TB, W), bf16),...  2.26 us
    pallas_call x1, Pallas kernels, per_device(): call(own_frame_kernel, (((FR, W), bf16), ((FR, W), bf16)), 2, vectors=5)  2.12 us
  transfers between devices with their start and end apart: 8, of which 5 were waited for; matrix products, arithmetic and copies ran while one was open for 1% of the time, Pallas kernels for 1%

profile of v1, /device:TPU:6, one launch (start us, length us, event | category | flops | bytes accessed | tf_op | source)
XLA Modules:
  0.0 88.8 jit_solution(9591453918680052893)
XLA Ops:
  0.6 1.2 %pack.1 = (bf16[512,384]{1,0:T(8,128)(2,1)S(1)}, bf16[128,384]{1,0:T(8,128)(2,1)S(1)}, bf16[128,384]{1,0:T(8,128)(2,1)S(1)}, f32[1,384]{1,0:T(1,128)S(1)}) custom-call(bf16[256,384]{1,0:T(8,128)(2,1)} %bitcast.8, bf16[256,384]{1,0:T(8,128)(2,1)} %bitcast.9, bf16[128,384]{1,0:T(8,128)(2,1)} %bitcast.10, bf16[128,384]{1,0:T(8,128)(2,1)} %bitcast.11, f32[384]{0:T(512)} %gain_ref.1), custom_call_target="tpu_custom_call" | custom-call | tf_op jit(solution)/shard_map/pack/pallas_call | solution.py:334
  1.8 1.3 %collective-permute-start.2 = (bf16[512,384]{1,0:T(8,128)(2,1)S(1)}, bf16[512,384]{1,0:T(8,128)(2,1)S(1)}, u32[]{:S(2)}, u32[]{:S(2)}) collective-permute-start(bf16[512,384]{1,0:T(8,128)(2,1)S(1)} %get-tuple-element.24.rest_0_.kv_ref), channel_id=1, source_target_pairs={{16,0},{24,8},{32,16},{40,24},{48,32},{56,40},{64,48},{72,56},{80,... | collective-permute-start | bytes 1179656 | tf_op jit(solution)/shard_map/ppermute | solution.py:28
  3.1 4.6 %collective-permute-start.1 = (bf16[512,384]{1,0:T(8,128)(2,1)S(1)}, bf16[512,384]{1,0:T(8,128)(2,1)S(1)}, u32[]{:S(2)}, u32[]{:S(2)}) collective-permute-start(bf16[512,384]{1,0:T(8,128)(2,1)S(1)} %get-tuple-element.24.rest_0_.kv_ref), channel_id=1, source_target_pairs={{0,16},{8,24},{16,32},{24,40},{32,48},{40,56},{48,64},{56,72},{64,... | collective-permute-start | bytes 1179656 | tf_op jit(solution)/shard_map/ppermute | solution.py:28
  7.7 1.9 %collective-permute-start = (bf16[512,384]{1,0:T(8,128)(2,1)S(1)}, bf16[512,384]{1,0:T(8,128)(2,1)S(1)}, u32[]{:S(2)}, u32[]{:S(2)}) collective-permute-start(bf16[512,384]{1,0:T(8,128)(2,1)S(1)} %get-tuple-element.24.rest_0_.kv_ref), channel_id=1, source_target_pairs={{0,8},{8,0},{16,24},{24,16},{32,40},{40,32},{48,56},{56,48},{64,72... | collective-permute-start | bytes 1179656 | tf_op jit(solution)/shard_map/ppermute | solution.py:28
  9.6 5.1 %collective-permute-done.2.rest_3_ = bf16[512,384]{1,0:T(8,128)(2,1)S(1)} collective-permute-done((bf16[512,384]{1,0:T(8,128)(2,1)S(1)}, bf16[512,384]{1,0:T(8,128)(2,1)S(1)}, u32[]{:S(2)}, u32[]{:S(2)}) %collective-permute-start.2) | collective-permute-done | bytes 393248 | tf_op jit(solution)/shard_map/ppermute | solution.py:28
  14.8 1.2 %collective-permute-done.1.rest_2_ = bf16[512,384]{1,0:T(8,128)(2,1)S(1)} collective-permute-done((bf16[512,384]{1,0:T(8,128)(2,1)S(1)}, bf16[512,384]{1,0:T(8,128)(2,1)S(1)}, u32[]{:S(2)}, u32[]{:S(2)}) %collective-permute-start.1) | collective-permute-done | bytes 393248 | tf_op jit(solution)/shard_map/ppermute | solution.py:28
  16.0 1.9 %collective-permute-start.3 = (bf16[512,384]{1,0:T(8,128)(2,1)S(1)}, bf16[512,384]{1,0:T(8,128)(2,1)S(1)}, u32[]{:S(2)}, u32[]{:S(2)}) collective-permute-start(bf16[512,384]{1,0:T(8,128)(2,1)S(1)} %broadcast_select_fusion), channel_id=1, source_target_pairs={{0,8},{8,0},{16,24},{24,16},{32,40},{40,32},{48,56},{56,48},{64,72... | collective-permute-start | bytes 1179656 | tf_op jit(solution)/shard_map/ppermute | solution.py:28
  19.2 0.0 collective-permute-done.rest_1_.kv_ref
  19.2 0.5 shard_map.110
  19.7 0.0 collective-permute-done.3.rest_4_
  19.7 1.4 %shard_map.111 = (f32[128,384]{1,0:T(8,128)S(1)}, f32[2,256,1280]{2,1,0:T(8,128)S(1)}, f32[8,2,128]{2,1,0:T(2,128)S(1)}, f32[8,128]{1,0:T(8,128)S(1)}) custom-call(s32[1,1]{1,0:T(1,128)S(6)} %copy.12.start_ref, s32[1,1]{1,0:T(1,128)S(6)} %copy.13.end_ref, bf16[128,384]{1,0:T(8,128)(2,1)S(1)} %get-tuple-element.21.q_ref, ...), custom_call_target="tpu_custom_call" | custom-call | flops 335544320 | bytes 4194304 | tf_op jit(solution)/shard_map/pallas_call | solution.py:364
  21.1 12.0 %all_to_all.10.stats_ref = f32[8,2,128]{2,1,0:T(2,128)S(1)} all-to-all(f32[8,2,128]{2,1,0:T(2,128)S(1)} %get-tuple-element.30), channel_id=1, replica_groups=mesh['dp'=2,'seq'=32,'tensor'=8] {'tensor'}, dimensions={0} | all-to-all | bytes 16384 | tf_op jit(solution)/shard_map/all_to_all | solution.py:371
  33.1 2.3 %shard_map.112 = (bf16[128,384]{1,0:T(8,128)(2,1)}, f32[32,1,384]{2,1,0:T(1,128)S(1)}, bf16[128,384]{1,0:T(8,128)(2,1)}, bf16[272,384]{1,0:T(8,128)(2,1)S(1)}) custom-call(s32[1,1]{1,0:T(1,128)S(6)} %copy.12.start_ref, s32[1,1]{1,0:T(1,128)S(6)} %copy.13.end_ref, bf16[128,384]{1,0:T(8,128)(2,1)S(1)} %get-tuple-element.21.q_ref, ...), custom_call_target="tpu_custom_call" | custom-call | flops 671088640 | bytes 4194304 | tf_op jit(solution)/shard_map/pallas_call | solution.py:372
  35.4 1.3 %collective-permute-start.5 = (bf16[272,384]{1,0:T(8,128)(2,1)S(1)}, bf16[272,384]{1,0:T(8,128)(2,1)S(1)}, u32[]{:S(2)}, u32[]{:S(2)}) collective-permute-start(bf16[272,384]{1,0:T(8,128)(2,1)S(1)} %get-tuple-element.33.sent_ref), channel_id=1, source_target_pairs={{16,0},{24,8},{32,16},{40,24},{48,32},{56,40},{64,48},{72,56},{80,... | collective-permute-start | bytes 626696 | tf_op jit(solution)/shard_map/ppermute | solution.py:28
  36.7 5.0 %collective-permute-start.4 = (bf16[272,384]{1,0:T(8,128)(2,1)S(1)}, bf16[272,384]{1,0:T(8,128)(2,1)S(1)}, u32[]{:S(2)}, u32[]{:S(2)}) collective-permute-start(bf16[272,384]{1,0:T(8,128)(2,1)S(1)} %get-tuple-element.33.sent_ref), channel_id=1, source_target_pairs={{0,16},{8,24},{16,32},{24,40},{32,48},{40,56},{48,64},{56,72},{64,... | collective-permute-start | bytes 626696 | tf_op jit(solution)/shard_map/ppermute | solution.py:28
  41.7 2.7 %collective-permute-done.5.above_ref = bf16[272,384]{1,0:T(8,128)(2,1)S(1)} collective-permute-done((bf16[272,384]{1,0:T(8,128)(2,1)S(1)}, bf16[272,384]{1,0:T(8,128)(2,1)S(1)}, u32[]{:S(2)}, u32[]{:S(2)}) %collective-permute-start.5) | collective-permute-done | bytes 208928 | tf_op jit(solution)/shard_map/ppermute | solution.py:28
  44.4 1.2 %collective-permute-done.4.below_ref = bf16[272,384]{1,0:T(8,128)(2,1)S(1)} collective-permute-done((bf16[272,384]{1,0:T(8,128)(2,1)S(1)}, bf16[272,384]{1,0:T(8,128)(2,1)S(1)}, u32[]{:S(2)}, u32[]{:S(2)}) %collective-permute-start.4) | collective-permute-done | bytes 208928 | tf_op jit(solution)/shard_map/ppermute | solution.py:28
  45.6 1.0 %shard_map.113 = bf16[512,384]{1,0:T(8,128)(2,1)S(1)} custom-call(bf16[512,384]{1,0:T(8,128)(2,1)S(1)} %collective-permute-done.rest_1_.kv_ref, bf16[272,384]{1,0:T(8,128)(2,1)S(1)} %get-tuple-element.33.sent_ref, bf16[272,384]{1,0:T(8,128)(2,1)S(1)} %collective-permute-done.4.below_ref, bf16[272,384]{1,0:T(8,128)(2,1)S(1)} %collective-permute-done.5.above_ref), custom_call_target="tpu_custom_call" | custom-call | flops 671088640 | bytes 4194304 | tf_op jit(solution)/shard_map/pallas_call | solution.py:385
  46.6 1.9 %collective-permute-start.6 = (bf16[512,384]{1,0:T(8,128)(2,1)S(1)}, bf16[512,384]{1,0:T(8,128)(2,1)S(1)}, u32[]{:S(2)}, u32[]{:S(2)}) collective-permute-start(bf16[512,384]{1,0:T(8,128)(2,1)S(1)} %shard_map.113), channel_id=1, source_target_pairs={{0,8},{8,0},{16,24},{24,16},{32,40},{40,32},{48,56},{56,48},{64,72... | collective-permute-start | bytes 1179656 | tf_op jit(solution)/shard_map/ppermute | solution.py:28
  48.5 32.0 %all_to_all.11 = f32[32,1,384]{2,1,0:T(1,128)S(1)} all-to-all(f32[32,1,384]{2,1,0:T(1,128)S(1)} %get-tuple-element.36), channel_id=1, replica_groups=mesh['dp'=2,'seq'=32,'tensor'=8] {'seq'}, dimensions={0} | all-to-all | bytes 98304 | tf_op jit(solution)/shard_map/all_to_all | solution.py:380
  80.5 0.1 reduce_sum.9
  80.6 2.7 %collective-permute-start.7 = (f32[384]{0:T(512)S(1)}, f32[384]{0:T(512)S(1)}, u32[]{:S(2)}, u32[]{:S(2)}) collective-permute-start(f32[384]{0:T(512)S(1)} %reduce_sum.9), channel_id=1, source_target_pairs={{0,256},{256,0},{1,257},{257,1},{2,258},{258,2},{3,259},{259,3},{4... | collective-permute-start | bytes 4616 | tf_op jit(solution)/shard_map/ppermute | solution.py:389
  83.4 2.7 %collective-permute-done.7 = f32[384]{0:T(512)S(1)} collective-permute-done((f32[384]{0:T(512)S(1)}, f32[384]{0:T(512)S(1)}, u32[]{:S(2)}, u32[]{:S(2)}) %collective-permute-start.7) | collective-permute-done | bytes 1568 | tf_op jit(solution)/shard_map/ppermute | solution.py:389
  86.1 0.6 add.3
  86.7 0.0 collective-permute-done.6.more_ref
  86.7 2.1 %shard_map.114 = (bf16[256,384]{1,0:T(8,128)(2,1)}, bf16[256,384]{1,0:T(8,128)(2,1)}) custom-call(bf16[512,384]{1,0:T(8,128)(2,1)S(1)} %get-tuple-element.24.rest_0_.kv_ref, bf16[272,384]{1,0:T(8,128)(2,1)S(1)} %get-tuple-element.33.sent_ref, bf16[272,384]{1,0:T(8,128)(2,1)S(1)} %collective-permute-done.4.below_ref, ...), custom_call_target="tpu_custom_call" | custom-call | flops 671088640 | bytes 4194304 | tf_op jit(solution)/shard_map/pallas_call | solution.py:390
  (1 shorter events, 0.0 us)
Async XLA Ops:
  1.8 12.9 %collective-permute-start.2 = (bf16[512,384]{1,0:T(8,128)(2,1)S(1)}, bf16[512,384]{1,0:T(8,128)(2,1)S(1)}, u32[]{:S(2)}, u32[]{:S(2)}) collective-permute-start(bf16[512,384]{1,0:T(8,128)(2,1)S(1)} %get-tuple-element.24.rest_0_.kv_ref), channel_id=1, source_target_pairs={{16,0},{24,8},{32,16},{40,24},{48,32},{56,40},{64,48},{72,56},{80,... | collective-permute-start | bytes 1179656 | tf_op jit(solution)/shard_map/ppermute | solution.py:28
  3.1 12.8 %collective-permute-start.1 = (bf16[512,384]{1,0:T(8,128)(2,1)S(1)}, bf16[512,384]{1,0:T(8,128)(2,1)S(1)}, u32[]{:S(2)}, u32[]{:S(2)}) collective-permute-start(bf16[512,384]{1,0:T(8,128)(2,1)S(1)} %get-tuple-element.24.rest_0_.kv_ref), channel_id=1, source_target_pairs={{0,16},{8,24},{16,32},{24,40},{32,48},{40,56},{48,64},{56,72},{64,... | collective-permute-start | bytes 1179656 | tf_op jit(solution)/shard_map/ppermute | solution.py:28
  7.7 11.5 %collective-permute-start = (bf16[512,384]{1,0:T(8,128)(2,1)S(1)}, bf16[512,384]{1,0:T(8,128)(2,1)S(1)}, u32[]{:S(2)}, u32[]{:S(2)}) collective-permute-start(bf16[512,384]{1,0:T(8,128)(2,1)S(1)} %get-tuple-element.24.rest_0_.kv_ref), channel_id=1, source_target_pairs={{0,8},{8,0},{16,24},{24,16},{32,40},{40,32},{48,56},{56,48},{64,72... | collective-permute-start | bytes 1179656 | tf_op jit(solution)/shard_map/ppermute | solution.py:28
  16.0 3.7 %collective-permute-start.3 = (bf16[512,384]{1,0:T(8,128)(2,1)S(1)}, bf16[512,384]{1,0:T(8,128)(2,1)S(1)}, u32[]{:S(2)}, u32[]{:S(2)}) collective-permute-start(bf16[512,384]{1,0:T(8,128)(2,1)S(1)} %broadcast_select_fusion), channel_id=1, source_target_pairs={{0,8},{8,0},{16,24},{24,16},{32,40},{40,32},{48,56},{56,48},{64,72... | collective-permute-start | bytes 1179656 | tf_op jit(solution)/shard_map/ppermute | solution.py:28
  35.4 9.1 %collective-permute-start.5 = (bf16[272,384]{1,0:T(8,128)(2,1)S(1)}, bf16[272,384]{1,0:T(8,128)(2,1)S(1)}, u32[]{:S(2)}, u32[]{:S(2)}) collective-permute-start(bf16[272,384]{1,0:T(8,128)(2,1)S(1)} %get-tuple-element.33.sent_ref), channel_id=1, source_target_pairs={{16,0},{24,8},{32,16},{40,24},{48,32},{56,40},{64,48},{72,56},{80,... | collective-permute-start | bytes 626696 | tf_op jit(solution)/shard_map/ppermute | solution.py:28
  36.7 8.9 %collective-permute-start.4 = (bf16[272,384]{1,0:T(8,128)(2,1)S(1)}, bf16[272,384]{1,0:T(8,128)(2,1)S(1)}, u32[]{:S(2)}, u32[]{:S(2)}) collective-permute-start(bf16[272,384]{1,0:T(8,128)(2,1)S(1)} %get-tuple-element.33.sent_ref), channel_id=1, source_target_pairs={{0,16},{8,24},{16,32},{24,40},{32,48},{40,56},{48,64},{56,72},{64,... | collective-permute-start | bytes 626696 | tf_op jit(solution)/shard_map/ppermute | solution.py:28
  46.6 40.1 %collective-permute-start.6 = (bf16[512,384]{1,0:T(8,128)(2,1)S(1)}, bf16[512,384]{1,0:T(8,128)(2,1)S(1)}, u32[]{:S(2)}, u32[]{:S(2)}) collective-permute-start(bf16[512,384]{1,0:T(8,128)(2,1)S(1)} %shard_map.113), channel_id=1, source_target_pairs={{0,8},{8,0},{16,24},{24,16},{32,40},{40,32},{48,56},{56,48},{64,72... | collective-permute-start | bytes 1179656 | tf_op jit(solution)/shard_map/ppermute | solution.py:28
  80.6 5.5 %collective-permute-start.7 = (f32[384]{0:T(512)S(1)}, f32[384]{0:T(512)S(1)}, u32[]{:S(2)}, u32[]{:S(2)}) collective-permute-start(f32[384]{0:T(512)S(1)} %reduce_sum.9), channel_id=1, source_target_pairs={{0,256},{256,0},{1,257},{257,1},{2,258},{258,2},{3,259},{259,3},{4... | collective-permute-start | bytes 4616 | tf_op jit(solution)/shard_map/ppermute | solution.py:389

commit v2 on v0

--- a/solution.py
+++ b/solution.py
@@ -363,10 +363,12 @@
         pltpu.with_memory_space_constraint(array, pltpu.HBM)
         for array in (keys[0], values[0], queries[0], grad_out[0], gain)
     ])
+    above = permute(own, "seq", lambda i: i - 2)
     below = permute(own, "seq", lambda i: i + 2)
-    above = permute(own, "seq", lambda i: i - 2)
     partner = permute(own, "seq", lambda i: i ^ 1)
-    asked = (query, permute(query, "seq", lambda i: i + 2), permute(query, "seq", lambda i: i - 2))
+    asked_above = permute(query, "seq", lambda i: i - 2)
+    asked_below = permute(query, "seq", lambda i: i + 2)
+    asked = (query, asked_below, asked_above)
     whole = (2 * TB, PIECES * FR)
     beyond = permute(jnp.where(core == 0, above, below), "seq", lambda i: i ^ 1)
     pieces = (own, partner, below, above, beyond)
@@ -395,7 +397,9 @@
     )(band_start, band_end, query, grad, gain_row, attn, probs, norms, stats, *pieces)
     spread = lax.all_to_all(gain_part, "seq", 0, 0, tiled=False)
     gain_sum = jnp.sum(spread, axis=(0, 1))
-    tokens = (sent, permute(sent, "seq", lambda i: i + 2), permute(sent, "seq", lambda i: i - 2))
+    tokens_above = permute(sent, "seq", lambda i: i - 2)
+    tokens_below = permute(sent, "seq", lambda i: i + 2)
+    tokens = (sent, tokens_below, tokens_above)
     (to_partner,) = call(
         partner_frame_kernel, (((2 * FR, W), bf16),), 2, vectors=7
     )(partner, *tokens, *asked)

time: 96.3 us -> 96.3 us (level)
  no operation moved by 1% of the time
where the time goes in v2:
time: 96.3 us; the launch traced here: 95.9 us
  blocking collectives  40.7 us (42%)
  starting transfers between devices  26.3 us (27%)
  waiting for transfers between devices  17.7 us (18%)
  Pallas kernels  8.41 us (9%)
  between operations  2.06 us (2%)
    all_to_all x1, blocking collectives, per_device(): spread = lax.all_to_all(gain_part, 'seq', 0, 0, tiled=False)  27.2 us
    ppermute x9, starting transfers between devices, permute(): return lax.ppermute(array, axis, pairs)  23 us
    ppermute x9, waiting for transfers between devices, permute(): return lax.ppermute(array, axis, pairs)  15.6 us
    all_to_all x1, blocking collectives, per_device(): stats = lax.all_to_all(stats, 'tensor', 0, 0, tiled=False)  13.5 us
    ppermute x1, starting transfers between devices, per_device(): gain_other = lax.ppermute(gain_sum, 'dp', [(0, 1), (1, 0)])  3.35 us
    pallas_call x1, Pallas kernels, per_device(): call(token_kernel, (((TB, W), bf16), ((SEQ, 1, W), f32), ((TB, W), bf16),...  2.26 us
    pallas_call x1, Pallas kernels, per_device(): call(own_frame_kernel, (((FR, W), bf16), ((FR, W), bf16)), 2, vectors=8)  2.12 us
    ppermute x1, waiting for transfers between devices, per_device(): gain_other = lax.ppermute(gain_sum, 'dp', [(0, 1), (1, 0)])  2.12 us
  transfers between devices with their start and end apart: 10, of which 5 were waited for; matrix products, arithmetic and copies ran while one was open for 1% of the time, Pallas kernels for 0%

profile of v2, /device:TPU:2, one launch (start us, length us, event | category | flops | bytes accessed | tf_op | source)
XLA Modules:
  0.0 95.9 jit_solution(15794282467774824112)
XLA Ops:
  0.6 1.2 %pack.1 = (bf16[512,384]{1,0:T(8,128)(2,1)S(1)}, bf16[128,384]{1,0:T(8,128)(2,1)S(1)}, bf16[128,384]{1,0:T(8,128)(2,1)S(1)}, f32[1,384]{1,0:T(1,128)S(1)}) custom-call(bf16[256,384]{1,0:T(8,128)(2,1)} %bitcast.8, bf16[256,384]{1,0:T(8,128)(2,1)} %bitcast.9, bf16[128,384]{1,0:T(8,128)(2,1)} %bitcast.10, bf16[128,384]{1,0:T(8,128)(2,1)} %bitcast.11, f32[384]{0:T(512)} %gain_ref.1), custom_call_target="tpu_custom_call" | custom-call | tf_op jit(solution)/shard_map/pack/pallas_call | solution.py:349
  1.8 3.8 %collective-permute-start.1 = (bf16[512,384]{1,0:T(8,128)(2,1)S(1)}, bf16[512,384]{1,0:T(8,128)(2,1)S(1)}, u32[]{:S(2)}, u32[]{:S(2)}) collective-permute-start(bf16[512,384]{1,0:T(8,128)(2,1)S(1)} %get-tuple-element.24.rest_0_.kv_ref), channel_id=1, source_target_pairs={{0,16},{8,24},{16,32},{24,40},{32,48},{40,56},{48,64},{56,72},{64,... | collective-permute-start | bytes 1179656 | tf_op jit(solution)/shard_map/ppermute | solution.py:28
  5.7 1.3 %collective-permute-start.2 = (bf16[512,384]{1,0:T(8,128)(2,1)S(1)}, bf16[512,384]{1,0:T(8,128)(2,1)S(1)}, u32[]{:S(2)}, u32[]{:S(2)}) collective-permute-start(bf16[512,384]{1,0:T(8,128)(2,1)S(1)} %get-tuple-element.24.rest_0_.kv_ref), channel_id=1, source_target_pairs={{16,0},{24,8},{32,16},{40,24},{48,32},{56,40},{64,48},{72,56},{80,... | collective-permute-start | bytes 1179656 | tf_op jit(solution)/shard_map/ppermute | solution.py:28
  7.0 1.9 %collective-permute-start = (bf16[512,384]{1,0:T(8,128)(2,1)S(1)}, bf16[512,384]{1,0:T(8,128)(2,1)S(1)}, u32[]{:S(2)}, u32[]{:S(2)}) collective-permute-start(bf16[512,384]{1,0:T(8,128)(2,1)S(1)} %get-tuple-element.24.rest_0_.kv_ref), channel_id=1, source_target_pairs={{0,8},{8,0},{16,24},{24,16},{32,40},{40,32},{48,56},{56,48},{64,72... | collective-permute-start | bytes 1179656 | tf_op jit(solution)/shard_map/ppermute | solution.py:28
  8.9 5.1 %collective-permute-done.1.rest_2_ = bf16[512,384]{1,0:T(8,128)(2,1)S(1)} collective-permute-done((bf16[512,384]{1,0:T(8,128)(2,1)S(1)}, bf16[512,384]{1,0:T(8,128)(2,1)S(1)}, u32[]{:S(2)}, u32[]{:S(2)}) %collective-permute-start.1) | collective-permute-done | bytes 393248 | tf_op jit(solution)/shard_map/ppermute | solution.py:28
  14.0 4.3 %collective-permute-done.2.rest_3_ = bf16[512,384]{1,0:T(8,128)(2,1)S(1)} collective-permute-done((bf16[512,384]{1,0:T(8,128)(2,1)S(1)}, bf16[512,384]{1,0:T(8,128)(2,1)S(1)}, u32[]{:S(2)}, u32[]{:S(2)}) %collective-permute-start.2) | collective-permute-done | bytes 393248 | tf_op jit(solution)/shard_map/ppermute | solution.py:28
  18.4 1.9 %collective-permute-start.3 = (bf16[512,384]{1,0:T(8,128)(2,1)S(1)}, bf16[512,384]{1,0:T(8,128)(2,1)S(1)}, u32[]{:S(2)}, u32[]{:S(2)}) collective-permute-start(bf16[512,384]{1,0:T(8,128)(2,1)S(1)} %broadcast_select_fusion), channel_id=1, source_target_pairs={{0,8},{8,0},{16,24},{24,16},{32,40},{40,32},{48,56},{56,48},{64,72... | collective-permute-start | bytes 1179656 | tf_op jit(solution)/shard_map/ppermute | solution.py:28
  21.6 0.0 collective-permute-done.rest_1_.kv_ref
  21.6 0.5 shard_map.110
  22.1 0.0 collective-permute-done.3.rest_4_
  22.1 1.4 %shard_map.111 = (f32[128,384]{1,0:T(8,128)S(1)}, f32[2,256,1280]{2,1,0:T(8,128)S(1)}, f32[8,2,128]{2,1,0:T(2,128)S(1)}, f32[8,128]{1,0:T(8,128)S(1)}) custom-call(s32[1,1]{1,0:T(1,128)S(6)} %copy.12.start_ref, s32[1,1]{1,0:T(1,128)S(6)} %copy.13.end_ref, bf16[128,384]{1,0:T(8,128)(2,1)S(1)} %get-tuple-element.21.q_ref, ...), custom_call_target="tpu_custom_call" | custom-call | flops 335544320 | bytes 4194304 | tf_op jit(solution)/shard_map/pallas_call | solution.py:382
  23.5 13.5 %all_to_all.10.stats_ref = f32[8,2,128]{2,1,0:T(2,128)S(1)} all-to-all(f32[8,2,128]{2,1,0:T(2,128)S(1)} %get-tuple-element.30), channel_id=1, replica_groups=mesh['dp'=2,'seq'=32,'tensor'=8] {'tensor'}, dimensions={0} | all-to-all | bytes 16384 | tf_op jit(solution)/shard_map/all_to_all | solution.py:389
  37.0 2.3 %shard_map.112 = (bf16[128,384]{1,0:T(8,128)(2,1)}, f32[32,1,384]{2,1,0:T(1,128)S(1)}, bf16[128,384]{1,0:T(8,128)(2,1)}, bf16[144,384]{1,0:T(8,128)(2,1)S(1)}) custom-call(s32[1,1]{1,0:T(1,128)S(6)} %copy.12.start_ref, s32[1,1]{1,0:T(1,128)S(6)} %copy.13.end_ref, bf16[128,384]{1,0:T(8,128)(2,1)S(1)} %get-tuple-element.21.q_ref, ...), custom_call_target="tpu_custom_call" | custom-call | flops 671088640 | bytes 4194304 | tf_op jit(solution)/shard_map/pallas_call | solution.py:390
  39.3 3.8 %collective-permute-start.4 = (bf16[144,384]{1,0:T(8,128)(2,1)S(1)}, bf16[144,384]{1,0:T(8,128)(2,1)S(1)}, u32[]{:S(2)}, u32[]{:S(2)}) collective-permute-start(bf16[144,384]{1,0:T(8,128)(2,1)S(1)} %get-tuple-element.33.sent_ref), channel_id=1, source_target_pairs={{0,16},{8,24},{16,32},{24,40},{32,48},{40,56},{48,64},{56,72},{64,... | collective-permute-start | bytes 331784 | tf_op jit(solution)/shard_map/ppermute | solution.py:28
  43.1 1.3 %collective-permute-start.5 = (bf16[144,384]{1,0:T(8,128)(2,1)S(1)}, bf16[144,384]{1,0:T(8,128)(2,1)S(1)}, u32[]{:S(2)}, u32[]{:S(2)}) collective-permute-start(bf16[144,384]{1,0:T(8,128)(2,1)S(1)} %get-tuple-element.33.sent_ref), channel_id=1, source_target_pairs={{16,0},{24,8},{32,16},{40,24},{48,32},{56,40},{64,48},{72,56},{80,... | collective-permute-start | bytes 331784 | tf_op jit(solution)/shard_map/ppermute | solution.py:28
  44.4 5.7 %collective-permute-start.6 = (bf16[128,384]{1,0:T(8,128)(2,1)S(1)}, bf16[128,384]{1,0:T(8,128)(2,1)S(1)}, u32[]{:S(2)}, u32[]{:S(2)}) collective-permute-start(bf16[128,384]{1,0:T(8,128)(2,1)S(1)} %get-tuple-element.21.q_ref), channel_id=1, source_target_pairs={{0,16},{8,24},{16,32},{24,40},{32,48},{40,56},{48,64},{56,72},{64,... | collective-permute-start | bytes 294920 | tf_op jit(solution)/shard_map/ppermute | solution.py:28
  50.1 1.3 %collective-permute-start.7 = (bf16[128,384]{1,0:T(8,128)(2,1)S(1)}, bf16[128,384]{1,0:T(8,128)(2,1)S(1)}, u32[]{:S(2)}, u32[]{:S(2)}) collective-permute-start(bf16[128,384]{1,0:T(8,128)(2,1)S(1)} %get-tuple-element.21.q_ref), channel_id=1, source_target_pairs={{16,0},{24,8},{32,16},{40,24},{48,32},{56,40},{64,48},{72,56},{80,... | collective-permute-start | bytes 294920 | tf_op jit(solution)/shard_map/ppermute | solution.py:28
  51.4 0.9 collective-permute-done.6.q_below_ref
  52.3 5.3 %collective-permute-done.7.q_above_ref = bf16[128,384]{1,0:T(8,128)(2,1)S(1)} collective-permute-done((bf16[128,384]{1,0:T(8,128)(2,1)S(1)}, bf16[128,384]{1,0:T(8,128)(2,1)S(1)}, u32[]{:S(2)}, u32[]{:S(2)}) %collective-permute-start.7) | collective-permute-done | bytes 98336 | tf_op jit(solution)/shard_map/ppermute | solution.py:28
  57.5 0.0 collective-permute-done.4.below_ref
  57.5 0.0 collective-permute-done.5.above_ref
  57.5 1.0 shard_map.113
  58.5 1.9 %collective-permute-start.8 = (bf16[512,384]{1,0:T(8,128)(2,1)S(1)}, bf16[512,384]{1,0:T(8,128)(2,1)S(1)}, u32[]{:S(2)}, u32[]{:S(2)}) collective-permute-start(bf16[512,384]{1,0:T(8,128)(2,1)S(1)} %shard_map.113), channel_id=1, source_target_pairs={{0,8},{8,0},{16,24},{24,16},{32,40},{40,32},{48,56},{56,48},{64,72... | collective-permute-start | bytes 1179656 | tf_op jit(solution)/shard_map/ppermute | solution.py:28
  60.4 27.2 %all_to_all.11 = f32[32,1,384]{2,1,0:T(1,128)S(1)} all-to-all(f32[32,1,384]{2,1,0:T(1,128)S(1)} %get-tuple-element.36), channel_id=1, replica_groups=mesh['dp'=2,'seq'=32,'tensor'=8] {'seq'}, dimensions={0} | all-to-all | bytes 98304 | tf_op jit(solution)/shard_map/all_to_all | solution.py:398
  87.6 0.1 reduce_sum.9
  87.7 3.3 %collective-permute-start.9 = (f32[384]{0:T(512)S(1)}, f32[384]{0:T(512)S(1)}, u32[]{:S(2)}, u32[]{:S(2)}) collective-permute-start(f32[384]{0:T(512)S(1)} %reduce_sum.9), channel_id=1, source_target_pairs={{0,256},{256,0},{1,257},{257,1},{2,258},{258,2},{3,259},{259,3},{4... | collective-permute-start | bytes 4616 | tf_op jit(solution)/shard_map/ppermute | solution.py:407
  91.0 2.1 %collective-permute-done.9 = f32[384]{0:T(512)S(1)} collective-permute-done((f32[384]{0:T(512)S(1)}, f32[384]{0:T(512)S(1)}, u32[]{:S(2)}, u32[]{:S(2)}) %collective-permute-start.9) | collective-permute-done | bytes 1568 | tf_op jit(solution)/shard_map/ppermute | solution.py:407
  93.2 0.6 add.3
  93.7 0.0 collective-permute-done.8.more_ref
  93.7 2.1 %shard_map.114 = (bf16[256,384]{1,0:T(8,128)(2,1)}, bf16[256,384]{1,0:T(8,128)(2,1)}) custom-call(bf16[512,384]{1,0:T(8,128)(2,1)S(1)} %get-tuple-element.24.rest_0_.kv_ref, bf16[144,384]{1,0:T(8,128)(2,1)S(1)} %get-tuple-element.33.sent_ref, bf16[144,384]{1,0:T(8,128)(2,1)S(1)} %collective-permute-done.4.below_ref, ...), custom_call_target="tpu_custom_call" | custom-call | flops 671088640 | bytes 4194304 | tf_op jit(solution)/shard_map/pallas_call | solution.py:408
  (1 shorter events, 0.0 us)
Async XLA Ops:
  1.8 12.2 %collective-permute-start.1 = (bf16[512,384]{1,0:T(8,128)(2,1)S(1)}, bf16[512,384]{1,0:T(8,128)(2,1)S(1)}, u32[]{:S(2)}, u32[]{:S(2)}) collective-permute-start(bf16[512,384]{1,0:T(8,128)(2,1)S(1)} %get-tuple-element.24.rest_0_.kv_ref), channel_id=1, source_target_pairs={{0,16},{8,24},{16,32},{24,40},{32,48},{40,56},{48,64},{56,72},{64,... | collective-permute-start | bytes 1179656 | tf_op jit(solution)/shard_map/ppermute | solution.py:28
  5.7 12.6 %collective-permute-start.2 = (bf16[512,384]{1,0:T(8,128)(2,1)S(1)}, bf16[512,384]{1,0:T(8,128)(2,1)S(1)}, u32[]{:S(2)}, u32[]{:S(2)}) collective-permute-start(bf16[512,384]{1,0:T(8,128)(2,1)S(1)} %get-tuple-element.24.rest_0_.kv_ref), channel_id=1, source_target_pairs={{16,0},{24,8},{32,16},{40,24},{48,32},{56,40},{64,48},{72,56},{80,... | collective-permute-start | bytes 1179656 | tf_op jit(solution)/shard_map/ppermute | solution.py:28
  7.0 14.6 %collective-permute-start = (bf16[512,384]{1,0:T(8,128)(2,1)S(1)}, bf16[512,384]{1,0:T(8,128)(2,1)S(1)}, u32[]{:S(2)}, u32[]{:S(2)}) collective-permute-start(bf16[512,384]{1,0:T(8,128)(2,1)S(1)} %get-tuple-element.24.rest_0_.kv_ref), channel_id=1, source_target_pairs={{0,8},{8,0},{16,24},{24,16},{32,40},{40,32},{48,56},{56,48},{64,72... | collective-permute-start | bytes 1179656 | tf_op jit(solution)/shard_map/ppermute | solution.py:28
  18.4 3.7 %collective-permute-start.3 = (bf16[512,384]{1,0:T(8,128)(2,1)S(1)}, bf16[512,384]{1,0:T(8,128)(2,1)S(1)}, u32[]{:S(2)}, u32[]{:S(2)}) collective-permute-start(bf16[512,384]{1,0:T(8,128)(2,1)S(1)} %broadcast_select_fusion), channel_id=1, source_target_pairs={{0,8},{8,0},{16,24},{24,16},{32,40},{40,32},{48,56},{56,48},{64,72... | collective-permute-start | bytes 1179656 | tf_op jit(solution)/shard_map/ppermute | solution.py:28
  39.3 18.2 %collective-permute-start.4 = (bf16[144,384]{1,0:T(8,128)(2,1)S(1)}, bf16[144,384]{1,0:T(8,128)(2,1)S(1)}, u32[]{:S(2)}, u32[]{:S(2)}) collective-permute-start(bf16[144,384]{1,0:T(8,128)(2,1)S(1)} %get-tuple-element.33.sent_ref), channel_id=1, source_target_pairs={{0,16},{8,24},{16,32},{24,40},{32,48},{40,56},{48,64},{56,72},{64,... | collective-permute-start | bytes 331784 | tf_op jit(solution)/shard_map/ppermute | solution.py:28
  43.1 14.4 %collective-permute-start.5 = (bf16[144,384]{1,0:T(8,128)(2,1)S(1)}, bf16[144,384]{1,0:T(8,128)(2,1)S(1)}, u32[]{:S(2)}, u32[]{:S(2)}) collective-permute-start(bf16[144,384]{1,0:T(8,128)(2,1)S(1)} %get-tuple-element.33.sent_ref), channel_id=1, source_target_pairs={{16,0},{24,8},{32,16},{40,24},{48,32},{56,40},{64,48},{72,56},{80,... | collective-permute-start | bytes 331784 | tf_op jit(solution)/shard_map/ppermute | solution.py:28
  44.4 7.9 %collective-permute-start.6 = (bf16[128,384]{1,0:T(8,128)(2,1)S(1)}, bf16[128,384]{1,0:T(8,128)(2,1)S(1)}, u32[]{:S(2)}, u32[]{:S(2)}) collective-permute-start(bf16[128,384]{1,0:T(8,128)(2,1)S(1)} %get-tuple-element.21.q_ref), channel_id=1, source_target_pairs={{0,16},{8,24},{16,32},{24,40},{32,48},{40,56},{48,64},{56,72},{64,... | collective-permute-start | bytes 294920 | tf_op jit(solution)/shard_map/ppermute | solution.py:28
  50.1 7.4 %collective-permute-start.7 = (bf16[128,384]{1,0:T(8,128)(2,1)S(1)}, bf16[128,384]{1,0:T(8,128)(2,1)S(1)}, u32[]{:S(2)}, u32[]{:S(2)}) collective-permute-start(bf16[128,384]{1,0:T(8,128)(2,1)S(1)} %get-tuple-element.21.q_ref), channel_id=1, source_target_pairs={{16,0},{24,8},{32,16},{40,24},{48,32},{56,40},{64,48},{72,56},{80,... | collective-permute-start | bytes 294920 | tf_op jit(solution)/shard_map/ppermute | solution.py:28
  58.5 35.2 %collective-permute-start.8 = (bf16[512,384]{1,0:T(8,128)(2,1)S(1)}, bf16[512,384]{1,0:T(8,128)(2,1)S(1)}, u32[]{:S(2)}, u32[]{:S(2)}) collective-permute-start(bf16[512,384]{1,0:T(8,128)(2,1)S(1)} %shard_map.113), channel_id=1, source_target_pairs={{0,8},{8,0},{16,24},{24,16},{32,40},{40,32},{48,56},{56,48},{64,72... | collective-permute-start | bytes 1179656 | tf_op jit(solution)/shard_map/ppermute | solution.py:28
  87.7 5.5 %collective-permute-start.9 = (f32[384]{0:T(512)S(1)}, f32[384]{0:T(512)S(1)}, u32[]{:S(2)}, u32[]{:S(2)}) collective-permute-start(f32[384]{0:T(512)S(1)} %reduce_sum.9), channel_id=1, source_target_pairs={{0,256},{256,0},{1,257},{257,1},{2,258},{258,2},{3,259},{259,3},{4... | collective-permute-start | bytes 4616 | tf_op jit(solution)/shard_map/ppermute | solution.py:407
